TPU v7x, 32 devices: a whole 2x2x4 slice. The times are simulated.
32 devices in a mesh: groups: 2 (over x), fsdp: 16 (over z, y, core).
Axes of the slice: x: 2, y: 2, z: 4, core: 2. Of those that a mesh axis runs over, the one named last changes fastest.
Arguments:
- layer_input: bfloat16 [512, 8192], P('groups', 'fsdp'), parts along dimension 0, may hold values from -6 to 6
- norm_gain: bfloat16 [8192], P('fsdp'), may hold values from 0.099609375 to 1.8984375
- w_query: bfloat16 [8192, 8192], P(None, 'fsdp'), may hold values from -0.0625 to 0.0625
- w_key: bfloat16 [8192, 1024], P('fsdp'), may hold values from -0.09375 to 0.09375
- w_value: bfloat16 [8192, 1024], P('fsdp'), may hold values from -0.09375 to 0.09375
- w_out: bfloat16 [8192, 8192], P('fsdp'), may hold values from -0.0625 to 0.0625
- cart_key: bfloat16 [4096, 1024], P(('groups', 'fsdp')), parts along dimension 0, may hold values from -100 to 100
- cart_value: bfloat16 [4096, 1024], P(('groups', 'fsdp')), parts along dimension 0, may hold values from -6 to 6
- grad_out: bfloat16 [512, 8192], P('groups', 'fsdp'), parts along dimension 0, may hold values from -6 to 6
Outputs:
- attn_out: bfloat16 [512, 8192], P('groups', 'fsdp'), parts along dimension 0
- grad_key: float32 [4096, 1024], P(('groups', 'fsdp')), parts along dimension 0
- grad_value: float32 [4096, 1024], P(('groups', 'fsdp')), parts along dimension 0
- new_keys: bfloat16 [512, 1024], P('groups', 'fsdp'), parts along dimension 0
- new_values: bfloat16 [512, 1024], P('groups', 'fsdp'), parts along dimension 0
There are 2 independent parts, one for each index of `groups`. A program takes and returns all parts, laid end to end along the dimension named above; an argument that names none is the same for every part. Nothing has to cross between parts.
All inputs are finite; a program needn't handle non-finite values.
Results may differ from a plain program's by a relative error of at most 0.015.
The roundings to bfloat16 on the way count: a program that leaves them out, or rounds other values in their place, can miss the bound.
Values may be sent and summed in bfloat16 or wider, within the bound.
A program may use at most 128 MiB of HBM per device.

v0:
```python
import jax
import jax.numpy as jnp
from jax import lax
from jax.sharding import PartitionSpec as P

H = 64
KV = 8
HD = 128
C = 2048
SEQ = 64


def rotate(vectors, positions):
    half_dim = vectors.shape[-1] // 2
    frequency = jnp.exp(
        -jnp.log(500000.0) * jnp.arange(half_dim, dtype=jnp.float32) * (2.0 / vectors.shape[-1])
    )
    angles = positions.astype(jnp.float32)[:, None] * frequency[None, :]
    cosines = jnp.cos(angles)[:, None, :]
    sine_table = jnp.sin(angles)[:, None, :]
    first_half = vectors[..., :half_dim]
    second = vectors[..., half_dim:]
    return jnp.concatenate(
        [first_half * cosines - second * sine_table, second * cosines + first_half * sine_table], -1
    )


def head_block(queries, slot_keys, slot_values, token_keys, token_values, grad_heads, seq_len):
    scaling = queries.shape[-1] ** (-0.5)
    token_count = queries.shape[1]
    score_cart = (
        jnp.einsum("gtd,cd->gtc", queries, slot_keys, preferred_element_type=jnp.float32) * scaling
    )
    score_tok = (
        jnp.einsum("gtd,sd->gts", queries, token_keys, preferred_element_type=jnp.float32) * scaling
    )
    index_rows = jnp.arange(token_count)
    causal = (index_rows[:, None] // seq_len == index_rows[None, :] // seq_len) & (
        index_rows[None, :] <= index_rows[:, None]
    )
    score_tok = jnp.where(causal[None], score_tok, -jnp.inf)
    row_max = jnp.maximum(
        jnp.max(score_cart, -1, keepdims=True), jnp.max(score_tok, -1, keepdims=True)
    )
    exp_cart = jnp.exp(score_cart - row_max)
    exp_tok = jnp.exp(score_tok - row_max)
    totals = jnp.sum(exp_cart, -1, keepdims=True) + jnp.sum(exp_tok, -1, keepdims=True)
    prob_cart = exp_cart / totals
    rounded_cart = prob_cart.astype(jnp.bfloat16)
    rounded_tok = (exp_tok / totals).astype(jnp.bfloat16)
    mixture = jnp.einsum(
        "gtc,cd->gtd", rounded_cart, slot_values, preferred_element_type=jnp.float32
    )
    mixture = mixture + jnp.einsum(
        "gts,sd->gtd", rounded_tok, token_values, preferred_element_type=jnp.float32
    )
    outputs = mixture.astype(jnp.bfloat16)
    grad_prob_cart = jnp.einsum(
        "gtd,cd->gtc", grad_heads, slot_values, preferred_element_type=jnp.float32
    )
    deltas = jnp.sum(
        grad_heads.astype(jnp.float32) * outputs.astype(jnp.float32), -1, keepdims=True
    )
    grad_score = (prob_cart * (grad_prob_cart - deltas)).astype(jnp.bfloat16)
    grad_keys = (
        jnp.einsum("gtc,gtd->cd", grad_score, queries, preferred_element_type=jnp.float32) * scaling
    )
    grad_values = jnp.einsum(
        "gtc,gtd->cd", rounded_cart, grad_heads, preferred_element_type=jnp.float32
    )
    return (outputs, grad_keys, grad_values)


def on_device(
    layer_input, norm_gain, w_query, w_key, w_value, w_out, cart_key, cart_value, grad_out
):
    devices = lax.axis_size("fsdp")
    my_index = lax.axis_index("fsdp")
    token_count = layer_input.shape[0]
    feature_count = layer_input.shape[1]
    local_heads = w_query.shape[1] // HD
    slot_count = cart_key.shape[0]
    kv_width = w_key.shape[1]
    gathered, gathered_gain = (
        lax.all_gather(layer_input, "fsdp", axis=1, tiled=True),
        lax.all_gather(norm_gain, "fsdp", axis=0, tiled=True),
    )
    gathered_f32 = gathered.astype(jnp.float32)
    inverse_rms = lax.rsqrt(jnp.mean(gathered_f32 * gathered_f32, -1, keepdims=True) + 1e-05)
    normed = (gathered_f32 * inverse_rms * gathered_gain.astype(jnp.float32)[None, :]).astype(
        jnp.bfloat16
    )
    own_part = lax.dynamic_slice_in_dim(normed, my_index * feature_count, feature_count, 1)
    partial_kv = jnp.concatenate(
        [
            jnp.dot(own_part, w_key, preferred_element_type=jnp.float32),
            jnp.dot(own_part, w_value, preferred_element_type=jnp.float32),
        ],
        1,
    )
    token_kv = lax.psum(partial_kv, "fsdp")
    positions = C + jnp.arange(token_count) % SEQ
    all_token_keys = (
        rotate(token_kv[:, :kv_width].reshape(token_count, kv_width // HD, HD), positions)
        .reshape(token_count, kv_width)
        .astype(jnp.bfloat16)
    )
    all_token_values = token_kv[:, kv_width:].astype(jnp.bfloat16)
    column_count = kv_width // devices
    new_keys = lax.dynamic_slice_in_dim(all_token_keys, my_index * column_count, column_count, 1)
    new_values = lax.dynamic_slice_in_dim(
        all_token_values, my_index * column_count, column_count, 1
    )
    kv_group = my_index * local_heads // (H // KV)
    token_keys = lax.dynamic_slice_in_dim(all_token_keys, kv_group * HD, HD, 1)
    token_values = lax.dynamic_slice_in_dim(all_token_values, kv_group * HD, HD, 1)
    queries = jnp.dot(normed, w_query, preferred_element_type=jnp.float32).reshape(
        token_count, local_heads, HD
    )
    queries = rotate(queries, positions).astype(jnp.bfloat16).transpose(1, 0, 2)
    spread_keys = jnp.repeat(cart_key.reshape(slot_count, KV, HD), devices // KV, axis=1)
    spread_values = jnp.repeat(cart_value.reshape(slot_count, KV, HD), devices // KV, axis=1)
    own_slots = lax.all_to_all(
        jnp.concatenate([spread_keys, spread_values], 2),
        "fsdp",
        split_axis=1,
        concat_axis=0,
        tiled=True,
    )
    slot_keys = own_slots[:, 0, :HD]
    slot_values = own_slots[:, 0, HD:]
    cotangent = lax.all_gather(grad_out, "fsdp", axis=1, tiled=True)
    grad_heads = lax.dot_general(
        cotangent, w_out, (((1,), (1,)), ((), ())), preferred_element_type=jnp.float32
    )
    grad_heads = (
        grad_heads.astype(jnp.bfloat16).reshape(token_count, local_heads, HD).transpose(1, 0, 2)
    )
    outputs, grad_keys, grad_values = head_block(
        queries, slot_keys, slot_values, token_keys, token_values, grad_heads, SEQ
    )
    head_outputs = outputs.transpose(1, 0, 2).reshape(token_count, local_heads * HD)
    partial_out = jnp.dot(head_outputs, w_out, preferred_element_type=jnp.float32)
    attn_out = lax.psum_scatter(partial_out, "fsdp", scatter_dimension=1, tiled=True).astype(
        jnp.bfloat16
    )
    total_slots = grad_keys.shape[0]
    stacked = jnp.concatenate([grad_keys, grad_values], 1).reshape(
        devices, total_slots // devices, 2 * HD
    )
    received = lax.all_to_all(stacked, "fsdp", split_axis=0, concat_axis=0, tiled=True)
    summed = jnp.sum(
        received.reshape(KV, devices // KV, total_slots // devices, 2 * HD), axis=1
    ).transpose(1, 0, 2)
    grad_key = summed[:, :, :HD].reshape(total_slots // devices, KV * HD)
    grad_value = summed[:, :, HD:].reshape(total_slots // devices, KV * HD)
    return (attn_out, grad_key, grad_value, new_keys, new_values)


def solution(mesh):
    return jax.shard_map(
        on_device,
        mesh=mesh,
        in_specs=(
            P("groups", "fsdp"),
            P("fsdp"),
            P(None, "fsdp"),
            P("fsdp", None),
            P("fsdp", None),
            P("fsdp", None),
            P(("groups", "fsdp"), None),
            P(("groups", "fsdp"), None),
            P("groups", "fsdp"),
        ),
        out_specs=(
            P("groups", "fsdp"),
            P(("groups", "fsdp"), None),
            P(("groups", "fsdp"), None),
            P("groups", "fsdp"),
            P("groups", "fsdp"),
        ),
        check_vma=False,
    )
```

profile of v0, /device:TPU:0, one launch (start us, length us, event | category | flops | bytes accessed | tf_op | source)
XLA Modules:
  0.0 399.3 jit_solution(2381138714927701704)
XLA Ops:
  8.7 1.0 copy_bitcast_fusion.4
  9.7 1.0 copy_bitcast_fusion.3
  10.9 1.1 pad_maximum_fusion.1
  12.0 7.4 %all-to-all-start = ((bf16[128,16,256]{2,0,1:T(8,128)(2,1)}), bf16[128,16,256]{2,0,1:T(8,128)(2,1)S(1)}, u32[]{:S(2)}, u32[]{:S(2)}) async-start(bf16[128,16,256]{2,0,1:T(8,128)(2,1)} %pad_maximum_fusion.1), calls=%async_computation | async-start | bytes 2097152 | tf_op jit(solution)/shard_map/all_to_all | solution.py:123
  20.1 40.6 %all-gather = bf16[16,1,512]{2,1,0:T(2,128)(2,1)S(1)} all-gather(bf16[1,1,512]{2,1,0:T(2,128)(2,1)S(1)} %reshape.259), channel_id=1, replica_groups=mesh['groups'=2,'fsdp'=16] {'fsdp'}, dimensions={0}, use_global_device_ids=true | all-gather | bytes 17408 | tf_op jit(solution)/shard_map/all_gather | solution.py:86
  61.4 17.4 %all-gather.4.cloned.1.call-done = bf16[256,8192]{1,0:T(8,128)(2,1)} async-done(((bf16[256,512]{1,0:T(8,128)(2,1)}), bf16[256,8192]{1,0:T(8,128)(2,1)}) %all-gather.4.cloned.1.call-update) | async-done | bytes 4194320 | tf_op jit(solution)/shard_map/all_gather | solution.py:85
  78.9 3.1 fusion
  82.0 3.6 fusion.2
  86.1 1.6 copy-done.3
  87.7 1.7 fusion.22
  89.4 1.5 pad_maximum_fusion
  91.2 7.0 %fusion.41 = f32[256,512]{1,0:T(8,128)S(1)} fusion(bf16[256,8192]{1,0:T(8,128)(2,1)} %copy-done.3, bf16[8192,512]{1,0:T(8,128)(2,1)} %param.11), kind=kOutput, calls=%fused_computation.77 | convolution fusion | flops 2147483648 | bytes 13107200 | tf_op jit(solution)/shard_map/dot_general | solution.py:117
  98.2 34.2 %all-gather.6.cloned.1.call-done = bf16[256,8192]{1,0:T(8,128)(2,1)} async-done(((bf16[256,512]{1,0:T(8,128)(2,1)}), bf16[256,8192]{1,0:T(8,128)(2,1)}) %all-gather.6.cloned.1.call-update) | async-done | bytes 4194320 | tf_op jit(solution)/shard_map/all_gather | solution.py:132
  132.4 7.0 %convolution_convert_fusion = bf16[256,512]{1,0:T(8,128)(2,1)S(1)} fusion(bf16[256,8192]{1,0:T(8,128)(2,1)} %all-gather.6.cloned.1.call-done, bf16[512,8192]{1,0:T(8,128)(2,1)} %param.14), kind=kOutput, calls=%fused_computation.24 | convolution fusion | flops 2147614720 | bytes 12845056 | tf_op jit(solution)/shard_map/dot_general | solution.py:133
  140.3 4.6 %multiply_reduce_fusion = (f32[4,256]{1,0:T(4,128)S(1)}, f32[4,256,2048]{2,1,0:T(8,128)}) fusion(bf16[2048,1,256]{2,0,1:T(8,128)(2,1)S(1)} %bitcast.97, bf16[256,4,64]{2,0,1:T(8,128)(2,1)S(1)} %get-tuple-element.21, bf16[256,4,64]{2,0,1:T(8,128)(2,1)S(1)} %get-tuple-element.20), kind=kOutput, calls=%fused_computation.7 | convolution fusion | flops 541588480 | bytes 9441280 | tf_op jit(solution)/shard_map/gtd,cd->gtc/dot_general | solution.py:32
  144.8 87.2 %all-reduce.2.cloned.1.call-done = f32[256,2048]{1,0:T(8,128)} async-done(((f32[256,2048]{1,0:T(8,128)}), f32[256,2048]{1,0:T(8,128)}) %all-reduce.2.cloned.1.call-update) | async-done | bytes 2097168 | tf_op jit(solution)/shard_map/psum | solution.py:101
  232.0 1.5 slice_bitcast_fusion
  235.9 1.9 fusion.4
  237.8 1.3 slice.63
  240.3 2.3 multiply_reduce_fusion.1
  243.5 5.8 %fusion.42 = f32[256,8192]{1,0:T(8,128)} fusion(bf16[256,512]{0,1:T(8,128)(2,1)S(1)} %bitcast.107, bf16[512,8192]{1,0:T(8,128)(2,1)S(1)} %bitcast.95), kind=kOutput, calls=%fused_computation.78 | convolution fusion | flops 2147483648 | bytes 17039360 | tf_op jit(solution)/shard_map/dot_general | solution.py:143
  249.3 5.6 %convolution_bitcast_fusion = f32[2048,128]{0,1:T(8,128)} fusion(bf16[4,256,128]{1,2,0:T(8,128)(2,1)S(1)} %bitcast.108, f32[4,256,2048]{2,1,0:T(8,128)} %get-tuple-element.31, f32[4,256]{1,0:T(4,128)S(1)} %add.115, f32[4,256]{1,0:T(4,128)S(1)} %max.8), kind=kOutput, calls=%fused_computation.10 | convolution fusion | flops 545259520 | bytes 9707520 | tf_op jit(solution)/shard_map/gtc,gtd->cd/dot_general | solution.py:68
  254.9 8.5 %fusion.5 = f32[2048,128]{0,1:T(8,128)} fusion(bf16[4,256,128]{1,2,0:T(8,128)(2,1)S(1)} %bitcast.109, f32[4,256]{1,0:T(4,128)S(1)} %get-tuple-element.34, bf16[2048,1,256]{2,0,1:T(8,128)(2,1)S(1)} %bitcast.99, bf16[256,4,64]{2,0,1:T(8,128)(2,1)S(1)} %get-tuple-element.21, bf16[256,4,64]{2,0,1:T(8,128)(2,1)S(1)} %get-tuple-element.20, ...), kind=kOutput, calls=%fused_computation.12 | convolution fusion | flops 1087111168 | bytes 10760192 | tf_op jit(solution)/shard_map/gtc,gtd->cd/dot_general | solution.py:66
  263.4 3.4 copy_bitcast_fusion
  266.8 3.8 all-to-all-start.1
  270.6 0.9 constant_dynamic-slice_fusion.1
  272.2 0.9 constant_dynamic-slice_fusion
  273.9 64.4 %all-to-all-done.1 = f32[16,128,256]{1,2,0:T(8,128)S(1)} async-done(((f32[16,128,256]{1,2,0:T(8,128)}), f32[16,128,256]{1,2,0:T(8,128)S(1)}, u32[]{:S(2)}, u32[]{:S(2)}) %all-to-all-start.1) | async-done | bytes 2097184 | tf_op jit(solution)/shard_map/all_to_all | solution.py:151
  339.2 1.0 copy.53
  340.3 1.0 copy.52
  341.3 49.7 %reduce-scatter.2.cloned.1.call-done = f32[256,512]{1,0:T(8,128)} async-done(((f32[256,8192]{1,0:T(8,128)}), f32[256,512]{1,0:T(8,128)}) %reduce-scatter.2.cloned.1.call-update) | async-done | bytes 524304 | tf_op jit(solution)/shard_map/reduce_scatter | solution.py:144
  391.0 1.8 convert_element_type.74
  (55 shorter events, 11.4 us)
Async XLA Ops:
  7.2 78.4 %copy-start = (bf16[512,1024]{1,0:T(8,128)(2,1)S(1)}, bf16[512,1024]{1,0:T(8,128)(2,1)}, u32[]{:S(2)}) copy-start(bf16[512,1024]{1,0:T(8,128)(2,1)} %param.13) | copy-start | bytes 3145732
  7.2 71.7 %all-gather.4.cloned.1.call-start = ((), (), s32[]{:S(2)}) async-start(), calls=%async_computation.3 | async-start | bytes 4456448 | tf_op jit(solution)/shard_map/all_gather | solution.py:85
  7.9 124.5 %all-gather.6.cloned.1.call-start = ((), (), s32[]{:S(2)}) async-start(), calls=%async_computation.6 | async-start | bytes 4456448 | tf_op jit(solution)/shard_map/all_gather | solution.py:132
  12.0 128.3 %all-to-all-start = ((bf16[128,16,256]{2,0,1:T(8,128)(2,1)}), bf16[128,16,256]{2,0,1:T(8,128)(2,1)S(1)}, u32[]{:S(2)}, u32[]{:S(2)}) async-start(bf16[128,16,256]{2,0,1:T(8,128)(2,1)} %pad_maximum_fusion.1), calls=%async_computation | async-start | bytes 2097152 | tf_op jit(solution)/shard_map/all_to_all | solution.py:123
  19.4 212.6 %all-reduce.2.cloned.1.call-start = ((), (), s32[]{:S(2)}) async-start(), calls=%async_computation.4 | async-start | bytes 4194304 | tf_op jit(solution)/shard_map/psum | solution.py:101
  85.6 2.1 copy-start.3
  91.0 300.0 %reduce-scatter.2.cloned.1.call-start = ((), (), s32[]{:S(2)}) async-start(), calls=%async_computation.5 | async-start | bytes 8912896 | tf_op jit(solution)/shard_map/reduce_scatter | solution.py:144
  232.0 3.9 copy-start.2
  234.5 0.8 copy-start.4
  239.1 0.8 copy-start.5
  239.9 2.7 slice-start
  240.3 3.2 slice-start.1
  263.4 129.4 %copy-start.1 = (bf16[512,1024]{1,0:T(8,128)(2,1)S(1)}, bf16[512,1024]{1,0:T(8,128)(2,1)}, u32[]{:S(2)}) copy-start(bf16[512,1024]{1,0:T(8,128)(2,1)} %param.13) | copy-start | bytes 3145732
  266.8 71.4 %all-to-all-start.1 = ((f32[16,128,256]{1,2,0:T(8,128)}), f32[16,128,256]{1,2,0:T(8,128)S(1)}, u32[]{:S(2)}, u32[]{:S(2)}) async-start(f32[16,128,256]{1,2,0:T(8,128)} %copy_bitcast_fusion), calls=%async_computation.2 | async-start | bytes 4194304 | tf_op jit(solution)/shard_map/all_to_all | solution.py:151
Sparse Core Ops, SparseCore 0:
  10.2 68.6 all-gather.3
  81.0 51.3 all-gather.5
  136.0 95.9 all-reduce.1
  249.4 141.5 reduce-scatter.1
where the time goes:
time: 400 us; the launch traced here: 399 us
  waiting for transfers between devices  254 us (64%)
  matrix products  43.7 us (11%)
  blocking collectives  40.6 us (10%)
  other arithmetic  18.3 us (5%)
  local copies, waits for them, and re-layouts  16.8 us (4%)
  between operations  14.1 us (4%)
  starting transfers between devices  11.5 us (3%)
    psum x1, waiting for transfers between devices, on_device(): token_kv = lax.psum(partial_kv, 'fsdp')  87.2 us
    all_to_all x1, waiting for transfers between devices, on_device(): lax.all_to_all(stacked, 'fsdp', split_axis=0, concat_axis=0, tiled=True)  64.4 us
    reduce_scatter x1, waiting for transfers between devices, on_device(): lax.psum_scatter(partial_out, 'fsdp', scatter_dimension=1, tiled=True)  49.7 us
    all_gather x1, blocking collectives, on_device(): lax.all_gather(norm_gain, 'fsdp', axis=0, tiled=True)  40.6 us
    all_gather x1, waiting for transfers between devices, on_device(): cotangent = lax.all_gather(grad_out, 'fsdp', axis=1, tiled=True)  34.2 us
    all_gather x1, waiting for transfers between devices, on_device(): lax.all_gather(layer_input, 'fsdp', axis=1, tiled=True)  17.4 us
    unnamed x25, local copies, waits for them, and re-layouts  10.6 us
    dot_general x1, matrix products, head_block(): jnp.einsum('gtc,gtd->cd', grad_score, queries, preferred_element_type=jnp...  8.53 us
  transfers between devices with their start and end apart: 6, of which 5 were waited for; matrix products, arithmetic and copies ran while one was open for 15% of the time, Pallas kernels for 0%

commit v1 on v0

--- a/solution.py
+++ b/solution.py
@@ -98,7 +98,7 @@
         ],
         1,
     )
-    token_kv = lax.psum(partial_kv, "fsdp")
+    token_kv = jnp.sum(lax.all_gather(partial_kv, "fsdp"), axis=0)
     positions = C + jnp.arange(token_count) % SEQ
     all_token_keys = (
         rotate(token_kv[:, :kv_width].reshape(token_count, kv_width // HD, HD), positions)

time: 400 us -> 487 us (1.22)
  waiting for transfers between devices: 254 us -> 346 us
  blocking collectives: 40.6 us -> 23.3 us
  other arithmetic: 18.3 us -> 34.5 us
    all_gather x0 -> x1, waiting for transfers between devices: none -> 149 us  [on_device(): token_kv = jnp.sum(lax.all_gather(partial_kv, 'fsdp'), axis=0)]
    psum x1 -> x0, waiting for transfers between devices: 87.2 us -> none  [on_device(): token_kv = lax.psum(partial_kv, 'fsdp')]
    all_gather x1, blocking collectives: 40.6 us -> 23.3 us  [on_device(): lax.all_gather(norm_gain, 'fsdp', axis=0, tiled=True)]
    all_gather x1, waiting for transfers between devices: 17.4 us -> 33.5 us  [on_device(): lax.all_gather(layer_input, 'fsdp', axis=1, tiled=True)]
    all_gather x1, waiting for transfers between devices: 34.2 us -> 47.6 us  [on_device(): cotangent = lax.all_gather(grad_out, 'fsdp', axis=1, tiled=True)]
    reduce_sum x0 -> x1, other arithmetic: none -> 12 us  [on_device(): token_kv = jnp.sum(lax.all_gather(partial_kv, 'fsdp'), axis=0)]
    unnamed x25 -> x43, local copies, waits for them, and re-layouts: 10.6 us -> 10 us
  transfers between devices with their start and end apart: 6 -> 6, of which waited for: 5 -> 5; matrix products, arithmetic and copies ran while one was open for 15% -> 12% of each run, Pallas kernels for 0% -> 0%
where the time goes in v1:
time: 487 us
  waiting for transfers between devices  346 us (71%)
  matrix products  46 us (9%)
  other arithmetic  34.5 us (7%)
  blocking collectives  23.3 us (5%)
  local copies, waits for them, and re-layouts  14.3 us (3%)
  between operations  14.2 us (3%)
  starting transfers between devices  8.51 us (2%)
    all_gather x1, waiting for transfers between devices, on_device(): token_kv = jnp.sum(lax.all_gather(partial_kv, 'fsdp'), axis=0)  149 us
    all_to_all x1, waiting for transfers between devices, on_device(): lax.all_to_all(stacked, 'fsdp', split_axis=0, concat_axis=0, tiled=True)  64.6 us
    reduce_scatter x1, waiting for transfers between devices, on_device(): lax.psum_scatter(partial_out, 'fsdp', scatter_dimension=1, tiled=True)  49.7 us
    all_gather x1, waiting for transfers between devices, on_device(): cotangent = lax.all_gather(grad_out, 'fsdp', axis=1, tiled=True)  47.6 us
    all_gather x1, waiting for transfers between devices, on_device(): lax.all_gather(layer_input, 'fsdp', axis=1, tiled=True)  33.5 us
    all_gather x1, blocking collectives, on_device(): lax.all_gather(norm_gain, 'fsdp', axis=0, tiled=True)  23.3 us
    reduce_sum x1, other arithmetic, on_device(): token_kv = jnp.sum(lax.all_gather(partial_kv, 'fsdp'), axis=0)  12 us
    unnamed x43, local copies, waits for them, and re-layouts  10 us
  transfers between devices with their start and end apart: 6, of which 5 were waited for; matrix products, arithmetic and copies ran while one was open for 12% of the time, Pallas kernels for 0%

profile of v1, /device:TPU:0, one launch (start us, length us, event | category | flops | bytes accessed | tf_op | source)
XLA Modules:
  0.0 486.6 jit_solution(9480537107470312706)
XLA Ops:
  9.4 23.3 %all-gather.1 = bf16[16,1,512]{2,1,0:T(2,128)(2,1)S(1)} all-gather(bf16[1,1,512]{2,1,0:T(2,128)(2,1)S(1)} %reshape.260), channel_id=1, replica_groups=mesh['groups'=2,'fsdp'=16] {'fsdp'}, dimensions={0}, use_global_device_ids=true | all-gather | bytes 17408 | tf_op jit(solution)/shard_map/all_gather | solution.py:86
  32.7 33.5 %all-gather.6.cloned.1.call-done = bf16[256,8192]{1,0:T(8,128)(2,1)} async-done(((bf16[256,512]{1,0:T(8,128)(2,1)}), bf16[256,8192]{1,0:T(8,128)(2,1)}) %all-gather.6.cloned.1.call-update) | async-done | bytes 4194320 | tf_op jit(solution)/shard_map/all_gather | solution.py:85
  66.2 3.1 fusion
  69.3 3.7 fusion.2
  73.5 1.5 copy-done.2
  75.5 1.6 pad_maximum_fusion
  77.4 1.1 pad_maximum_fusion.1
  78.5 3.7 all-to-all-start
  83.5 47.6 %all-gather.8.cloned.1.call-done = bf16[256,8192]{1,0:T(8,128)(2,1)} async-done(((bf16[256,512]{1,0:T(8,128)(2,1)}), bf16[256,8192]{1,0:T(8,128)(2,1)}) %all-gather.8.cloned.1.call-update) | async-done | bytes 4194320 | tf_op jit(solution)/shard_map/all_gather | solution.py:132
  131.2 7.0 %convolution_convert_fusion = bf16[256,512]{1,0:T(8,128)(2,1)S(1)} fusion(bf16[256,8192]{1,0:T(8,128)(2,1)} %all-gather.8.cloned.1.call-done, bf16[512,8192]{1,0:T(8,128)(2,1)} %param.14), kind=kOutput, calls=%fused_computation.24 | convolution fusion | flops 2147614720 | bytes 12845056 | tf_op jit(solution)/shard_map/dot_general | solution.py:133
  139.0 8.3 %fusion.41 = f32[256,512]{1,0:T(8,128)S(1)} fusion(bf16[256,8192]{1,0:T(8,128)(2,1)} %copy-done.2, bf16[8192,512]{1,0:T(8,128)(2,1)} %param.11), kind=kOutput, calls=%fused_computation.76 | convolution fusion | flops 2147483648 | bytes 13107200 | tf_op jit(solution)/shard_map/dot_general | solution.py:117
  148.1 4.5 multiply_reduce_fusion
  152.6 148.9 %all-gather.10.cloned.1.call-done = f32[4096,2048]{1,0:T(8,128)} async-done(((f32[256,2048]{1,0:T(8,128)}), f32[4096,2048]{1,0:T(8,128)}) %all-gather.10.cloned.1.call-update) | async-done | bytes 33554448 | tf_op jit(solution)/shard_map/all_gather | solution.py:101
  301.5 12.0 %reduce_sum.55 = f32[256,2048]{1,0:T(8,128)S(1)} reduce(f32[16,256,2048]{2,1,0:T(8,128)} %bitcast.94, f32[]{:T(128)} %constant.68.clone.1), dimensions={0}, to_apply=%region_2.3 | reduce | flops 7864320 | bytes 35651588 | tf_op jit(solution)/shard_map/reduce_sum | solution.py:101
  313.6 1.0 slice_bitcast_fusion
  314.7 1.0 copy.62
  315.7 1.4 copy.66
  317.1 1.4 subtract_convert_fusion
  319.7 1.9 fusion.40
  321.8 4.4 fusion.4
  326.2 1.3 fusion.18
  327.6 2.3 multiply_reduce_fusion.1
  330.0 5.8 %fusion.42 = f32[256,8192]{1,0:T(8,128)} fusion(bf16[256,512]{0,1:T(8,128)(2,1)S(1)} %bitcast.111, bf16[512,8192]{1,0:T(8,128)(2,1)S(1)} %bitcast.99), kind=kOutput, calls=%fused_computation.77 | convolution fusion | flops 2147483648 | bytes 17039360 | tf_op jit(solution)/shard_map/dot_general | solution.py:143
  335.8 5.6 %convolution_bitcast_fusion = f32[2048,128]{0,1:T(8,128)} fusion(bf16[4,256,128]{1,2,0:T(8,128)(2,1)S(1)} %bitcast.112, f32[4,256,2048]{2,1,0:T(8,128)} %get-tuple-element.31, f32[4,256]{1,0:T(4,128)S(1)} %add.113, f32[4,256]{1,0:T(4,128)S(1)} %max.8), kind=kOutput, calls=%fused_computation.10 | convolution fusion | flops 545259520 | bytes 9707520 | tf_op jit(solution)/shard_map/gtc,gtd->cd/dot_general | solution.py:68
  341.4 8.3 %fusion.5 = f32[2048,128]{0,1:T(8,128)} fusion(bf16[4,256,128]{1,2,0:T(8,128)(2,1)S(1)} %bitcast.113, f32[4,256]{1,0:T(4,128)S(1)} %get-tuple-element.34, bf16[2048,1,256]{2,0,1:T(8,128)(2,1)S(1)} %bitcast.103, bf16[256,4,64]{2,0,1:T(8,128)(2,1)S(1)} %copy-done.4, bf16[256,4,64]{2,0,1:T(8,128)(2,1)S(1)} %get-tuple-element.20, ...), kind=kOutput, calls=%fused_computation.12 | convolution fusion | flops 1087111168 | bytes 10760192 | tf_op jit(solution)/shard_map/gtc,gtd->cd/dot_general | solution.py:66
  349.7 3.5 copy_bitcast_fusion
  353.2 4.7 all-to-all-start.1
  359.6 1.4 constant_dynamic-slice_fusion
  360.9 64.6 %all-to-all-done.1 = f32[16,128,256]{1,2,0:T(8,128)S(1)} async-done(((f32[16,128,256]{1,2,0:T(8,128)}), f32[16,128,256]{1,2,0:T(8,128)S(1)}, u32[]{:S(2)}, u32[]{:S(2)}) %all-to-all-start.1) | async-done | bytes 2097184 | tf_op jit(solution)/shard_map/all_to_all | solution.py:151
  426.5 1.0 copy.52
  428.6 49.7 %reduce-scatter.2.cloned.1.call-done = f32[256,512]{1,0:T(8,128)} async-done(((f32[256,8192]{1,0:T(8,128)}), f32[256,512]{1,0:T(8,128)}) %reduce-scatter.2.cloned.1.call-update) | async-done | bytes 524304 | tf_op jit(solution)/shard_map/reduce_scatter | solution.py:144
  478.3 1.8 convert_element_type.74
  (75 shorter events, 11.4 us)
Async XLA Ops:
  7.2 65.9 %copy-start = (bf16[512,1024]{1,0:T(8,128)(2,1)S(1)}, bf16[512,1024]{1,0:T(8,128)(2,1)}, u32[]{:S(2)}) copy-start(bf16[512,1024]{1,0:T(8,128)(2,1)} %param.13) | copy-start | bytes 3145732
  7.2 67.8 %copy-start.8 = (bf16[512,1024]{1,0:T(8,128)(2,1)S(1)}, bf16[512,1024]{1,0:T(8,128)(2,1)}, u32[]{:S(2)}) copy-start(bf16[512,1024]{1,0:T(8,128)(2,1)} %param.12) | copy-start | bytes 3145732
  7.2 59.0 %all-gather.6.cloned.1.call-start = ((), (), s32[]{:S(2)}) async-start(), calls=%async_computation.3 | async-start | bytes 4456448 | tf_op jit(solution)/shard_map/all_gather | solution.py:85
  7.9 123.2 %all-gather.8.cloned.1.call-start = ((), (), s32[]{:S(2)}) async-start(), calls=%async_computation.5 | async-start | bytes 4456448 | tf_op jit(solution)/shard_map/all_gather | solution.py:132
  8.7 292.8 %all-gather.10.cloned.1.call-start = ((), (), s32[]{:S(2)}) async-start(), calls=%async_computation.6 | async-start | bytes 35651584 | tf_op jit(solution)/shard_map/all_gather | solution.py:101
  69.3 7.7 %copy-start.10 = (bf16[128,1024]{1,0:T(8,128)(2,1)S(1)}, bf16[128,1024]{1,0:T(8,128)(2,1)}, u32[]{:S(2)}) copy-start(bf16[128,1024]{1,0:T(8,128)(2,1)} %param.15) | copy-start | bytes 786436
  69.3 7.8 %copy-start.11 = (bf16[128,1024]{1,0:T(8,128)(2,1)S(1)}, bf16[128,1024]{1,0:T(8,128)(2,1)}, u32[]{:S(2)}) copy-start(bf16[128,1024]{1,0:T(8,128)(2,1)} %param.16) | copy-start | bytes 786436
  73.0 2.0 copy-start.2
  78.5 69.6 %all-to-all-start = ((bf16[128,16,256]{2,0,1:T(8,128)(2,1)}), bf16[128,16,256]{2,0,1:T(8,128)(2,1)S(1)}, u32[]{:S(2)}, u32[]{:S(2)}) async-start(bf16[128,16,256]{2,0,1:T(8,128)(2,1)} %pad_maximum_fusion.1), calls=%async_computation | async-start | bytes 2097152 | tf_op jit(solution)/shard_map/all_to_all | solution.py:123
  82.2 396.1 %reduce-scatter.2.cloned.1.call-start = ((), (), s32[]{:S(2)}) async-start(), calls=%async_computation.4 | async-start | bytes 8912896 | tf_op jit(solution)/shard_map/reduce_scatter | solution.py:144
  83.5 64.4 %copy-start.7 = (f32[256,64]{1,0:T(8,128)}, f32[256,64]{1,0:T(8,128)S(1)}, u32[]{:S(2)}) copy-start(f32[256,64]{1,0:T(8,128)S(1)} %get-tuple-element.29) | copy-start | bytes 196612
  148.0 165.5 %copy-start.3 = (bf16[256,4,64]{2,0,1:T(8,128)(2,1)}, bf16[256,4,64]{2,0,1:T(8,128)(2,1)S(1)}, u32[]{:S(2)}) copy-start(bf16[256,4,64]{2,0,1:T(8,128)(2,1)S(1)} %get-tuple-element.21) | copy-start | bytes 393220
  148.1 153.5 %copy-start.5 = (bf16[128,16,256]{2,0,1:T(8,128)(2,1)}, bf16[128,16,256]{2,0,1:T(8,128)(2,1)S(1)}, u32[]{:S(2)}) copy-start(bf16[128,16,256]{2,0,1:T(8,128)(2,1)S(1)} %all-to-all-done) | copy-start | bytes 3145732
  314.7 5.0 %copy-start.4 = (bf16[256,4,64]{2,0,1:T(8,128)(2,1)S(1)}, bf16[256,4,64]{2,0,1:T(8,128)(2,1)}, u32[]{:S(2)}) copy-start(bf16[256,4,64]{2,0,1:T(8,128)(2,1)} %copy-done.3) | copy-start | bytes 393220
  318.8 8.8 %slice-start = ((s8[8388608]{0:T(1024)(128)(4,1)}), s8[4194304]{0:T(1024)(128)(4,1)S(1)}, s32[]{:S(2)}) async-start(s8[8388608]{0:T(1024)(128)(4,1)} %bitcast.95), calls=%async_computation.7 | async-start | bytes 8388608
  318.8 8.8 %copy-start.6 = (bf16[128,16,256]{2,0,1:T(8,128)(2,1)S(1)}, bf16[128,16,256]{2,0,1:T(8,128)(2,1)}, u32[]{:S(2)}) copy-start(bf16[128,16,256]{2,0,1:T(8,128)(2,1)} %copy-done.5) | copy-start | bytes 3145732
  318.8 8.8 %copy-start.12 = (bf16[256,512]{0,1:T(8,128)(2,1)S(1)}, bf16[256,512]{0,1:T(8,128)(2,1)}, u32[]{:S(2)}) copy-start(bf16[256,512]{0,1:T(8,128)(2,1)} %copy.44) | copy-start | bytes 786436
  318.9 0.8 copy-start.9
  321.8 5.8 %slice-start.1 = ((s8[8388608]{0:T(1024)(128)(4,1)}), s8[4194304]{0:T(1024)(128)(4,1)S(1)}, s32[]{:S(2)}) async-start(s8[8388608]{0:T(1024)(128)(4,1)} %bitcast.95), calls=%async_computation.8 | async-start | bytes 8388608
  326.2 3.7 slice-start.2
  327.6 2.4 slice-start.3
  349.7 130.3 %copy-start.1 = (bf16[512,1024]{1,0:T(8,128)(2,1)S(1)}, bf16[512,1024]{1,0:T(8,128)(2,1)}, u32[]{:S(2)}) copy-start(bf16[512,1024]{1,0:T(8,128)(2,1)} %param.13) | copy-start | bytes 3145732
  353.2 72.4 %all-to-all-start.1 = ((f32[16,128,256]{1,2,0:T(8,128)}), f32[16,128,256]{1,2,0:T(8,128)S(1)}, u32[]{:S(2)}, u32[]{:S(2)}) async-start(f32[16,128,256]{1,2,0:T(8,128)} %copy_bitcast_fusion), calls=%async_computation.2 | async-start | bytes 4194304 | tf_op jit(solution)/shard_map/all_to_all | solution.py:151
Sparse Core Ops, SparseCore 0:
  10.2 55.9 all-gather.5
  68.4 62.7 all-gather.7
  132.8 168.7 all-gather.9
  335.9 142.3 reduce-scatter.1
